TPU v7x, 512 devices: a whole 4x4x16 slice. The times are simulated.
512 devices in a mesh: seq: 32 (over y, x, core), head: 16 (over z).
Axes of the slice: x: 4, y: 4, z: 16, core: 2. Of those that a mesh axis runs over, the one named last changes fastest.
Arguments:
- queries: bfloat16 [4096, 2048], P('seq', 'head'), may hold values from -6 to 6
- keys: bfloat16 [4096, 2048], P('seq', 'head'), may hold values from -6 to 6
- values: bfloat16 [4096, 4096], P('seq', 'head'), may hold values from -6 to 6
- gate_code: int32 [4096, 32], P('seq', 'head'), may hold values from 1 to 1000
- beta_code: int32 [4096, 32], P('seq', 'head'), may hold values from 1 to 255
- out_grad: bfloat16 [4096, 2048], P('seq', 'head'), may hold values from -6 to 6
- w_out: bfloat16 [4096, 2048], P('head'), may hold values from -0.09375 to 0.09375
Outputs:
- attn_out: bfloat16 [4096, 4096], P('seq', 'head')
- q_grad: float32 [4096, 2048], P('seq', 'head')
- k_grad: float32 [4096, 2048], P('seq', 'head')
- v_grad: float32 [4096, 4096], P('seq', 'head')
- weight_grad: float32 [4096, 2048], P(('head', 'seq'))
All inputs are finite; a program needn't handle non-finite values.
Results may differ from a plain program's by a relative error of at most 0.0029.
Values may be sent and summed in bfloat16 or wider, within the bound.
No kernel may reach another device: no remote copies, remote signals or barrier semaphores. Data moves between devices by JAX's collectives and lax.ppermute only.
A program may use at most 64 MiB of HBM per device.

v0:
```python
import jax
import jax.numpy as jnp
from jax import lax
from jax.sharding import PartitionSpec as P

HEAD_DIM = 128
SPAN = 64
norm_eps = 1e-06
gate_step = 1e-06
beta_steps = 256.0
highest = lax.Precision.HIGHEST


def from_behind(value, axis, steps):
    count = lax.axis_size(axis)
    initial, last = (max(0, -steps), min(count, count - steps))
    return lax.ppermute(value, axis, [(source, source + steps) for source in range(initial, last)])


def normalize(block_rows):
    return block_rows * lax.rsqrt(
        jnp.sum(block_rows * block_rows, axis=-1, keepdims=True) + norm_eps
    )


def block_masks(block):
    row_ids = lax.broadcasted_iota(jnp.int32, (block, block), 0)
    col_ids = lax.broadcasted_iota(jnp.int32, (block, block), 1)
    return (row_ids > col_ids, row_ids >= col_ids)


def span_pass(query_blocks, key_blocks, value_blocks, decay_blocks, beta_blocks, state):
    strict, inclusive = block_masks(query_blocks.shape[1])

    def span_advance(state, pieces):
        query_block, key_block, value_block, decay_log, beta_block = pieces
        log_cum = jnp.cumsum(decay_log)
        decay_cum = jnp.exp(log_cum)
        ratio = jnp.exp(log_cum[:, None] - log_cum[None, :]) * beta_block[None, :]
        key_gram = jnp.dot(key_block, key_block.T, precision=highest)
        query_key = jnp.dot(query_block, key_block.T, precision=highest)
        lower_mix = jnp.where(strict, ratio * key_gram, 0.0)
        out_mix = jnp.where(inclusive, ratio * query_key, 0.0)
        right_side = value_block - decay_cum[:, None] * jnp.dot(key_block, state, precision=highest)
        new_values = lax.linalg.triangular_solve(
            lower_mix, right_side, left_side=True, lower=True, unit_diagonal=True
        )
        outputs = decay_cum[:, None] * jnp.dot(query_block, state, precision=highest) + jnp.dot(
            out_mix, new_values, precision=highest
        )
        weights = beta_block * jnp.exp(log_cum[-1] - log_cum)
        next_state = decay_cum[-1] * state + jnp.dot(
            key_block.T, weights[:, None] * new_values, precision=highest
        )
        return (next_state, outputs)

    final_state, outputs = lax.scan(
        span_advance, state, (query_blocks, key_blocks, value_blocks, decay_blocks, beta_blocks)
    )
    return (outputs, final_state)


def head_forward(query_head, key_head, value_pair, decay_pair, beta_pair, start_pair):
    length, width = query_head.shape
    blocks = length // SPAN
    query_blocks = (normalize(query_head) * width ** (-0.5)).reshape(blocks, SPAN, width)
    key_blocks = normalize(key_head).reshape(blocks, SPAN, width)

    def head_single(value_head, decay_head, beta_head, start_state):
        outputs, final_state = span_pass(
            query_blocks,
            key_blocks,
            value_head.reshape(blocks, SPAN, width),
            decay_head.reshape(blocks, SPAN),
            beta_head.reshape(blocks, SPAN),
            start_state,
        )
        return (outputs.reshape(length, width), final_state)

    return jax.vmap(head_single)(value_pair, decay_pair, beta_pair, start_pair)


def slab_effect(key_head, value_pair, decay_pair, beta_pair):
    length, width = key_head.shape
    blocks = length // SPAN
    key_blocks = normalize(key_head).reshape(blocks, SPAN, width)
    strict, inclusive = block_masks(SPAN)

    def slab_single(value_head, decay_head, beta_head):

        def single_advance(carried, pieces):
            state, transition = carried
            key_block, value_block, decay_log, beta_block = pieces
            log_cum = jnp.cumsum(decay_log)
            decay_cum = jnp.exp(log_cum)
            ratio = jnp.exp(log_cum[:, None] - log_cum[None, :]) * beta_block[None, :]
            key_gram = jnp.dot(key_block, key_block.T, precision=highest)
            lower_mix = jnp.where(strict, ratio * key_gram, 0.0)
            stacked = jnp.concatenate([value_block, decay_cum[:, None] * key_block], axis=1)
            solved = lax.linalg.triangular_solve(
                lower_mix, stacked, left_side=True, lower=True, unit_diagonal=True
            )
            new_values = solved[:, :width]
            mixed_keys = solved[:, width:]
            weights = beta_block * jnp.exp(log_cum[-1] - log_cum)
            weighted_keys = key_block * weights[:, None]
            next_state = decay_cum[-1] * state + jnp.dot(
                weighted_keys.T,
                new_values - jnp.dot(mixed_keys, state, precision=highest),
                precision=highest,
            )
            next_transition = decay_cum[-1] * transition - jnp.dot(
                weighted_keys.T,
                jnp.dot(mixed_keys, transition, precision=highest),
                precision=highest,
            )
            return ((next_state, next_transition), None)

        start_carry = (jnp.zeros((width, width), jnp.float32), jnp.eye(width, dtype=jnp.float32))
        (state, transition), unused = lax.scan(
            single_advance,
            start_carry,
            (
                key_blocks,
                value_head.reshape(blocks, SPAN, width),
                decay_head.reshape(blocks, SPAN),
                beta_head.reshape(blocks, SPAN),
            ),
        )
        return (transition, state)

    return jax.vmap(slab_single)(value_pair, decay_pair, beta_pair)


def start_adjoint(query_head, key_head, decay_pair, beta_pair, cot_pair):
    length, width = query_head.shape
    blocks = length // SPAN
    query_blocks = (normalize(query_head) * width ** (-0.5)).reshape(blocks, SPAN, width)
    key_blocks = normalize(key_head).reshape(blocks, SPAN, width)
    strict, inclusive = block_masks(SPAN)

    def start_single(decay_head, beta_head, cot_head):

        def retreat(grad_state, pieces):
            query_block, key_block, decay_log, beta_block, cot_block = pieces
            log_cum = jnp.cumsum(decay_log)
            decay_cum = jnp.exp(log_cum)
            ratio = jnp.exp(log_cum[:, None] - log_cum[None, :]) * beta_block[None, :]
            key_gram = jnp.dot(key_block, key_block.T, precision=highest)
            query_key = jnp.dot(query_block, key_block.T, precision=highest)
            lower_mix = jnp.where(strict, ratio * key_gram, 0.0)
            out_mix = jnp.where(inclusive, ratio * query_key, 0.0)
            mixed_keys = lax.linalg.triangular_solve(
                lower_mix,
                decay_cum[:, None] * key_block,
                left_side=True,
                lower=True,
                unit_diagonal=True,
            )
            weights = beta_block * jnp.exp(log_cum[-1] - log_cum)
            weighted_keys = key_block * weights[:, None]
            probe = decay_cum[:, None] * query_block - jnp.dot(
                out_mix, mixed_keys, precision=highest
            )
            through = decay_cum[-1] * grad_state - jnp.dot(
                mixed_keys.T,
                jnp.dot(weighted_keys, grad_state, precision=highest),
                precision=highest,
            )
            return (jnp.dot(probe.T, cot_block, precision=highest) + through, None)

        zeros_state = jnp.zeros((width, width), jnp.float32)
        result, unused = lax.scan(
            retreat,
            zeros_state,
            (
                query_blocks,
                key_blocks,
                decay_head.reshape(blocks, SPAN),
                beta_head.reshape(blocks, SPAN),
                cot_head.reshape(blocks, SPAN, width),
            ),
            reverse=True,
        )
        return result

    return jax.vmap(start_single)(decay_pair, beta_pair, cot_pair)


def matmul_states(left, right):
    return jnp.einsum("abij,abjk->abik", left, right, precision=highest)


def final_pass(
    query_head, key_head, value_pair, decay_pair, beta_pair, start_pair, cot_pair, end_pair
):

    def forward(query_in, key_in, value_in):
        return head_forward(query_in, key_in, value_in, decay_pair, beta_pair, start_pair)

    (core_out, final_unused), pullback = jax.vjp(forward, query_head, key_head, value_pair)
    return (core_out,) + pullback((cot_pair, end_pair))


def per_device(queries, keys, values, gate_code, beta_code, out_grad, w_out):
    length = queries.shape[0]
    width = HEAD_DIM
    key_count = queries.shape[1] // width
    group = values.shape[1] // queries.shape[1]
    query_heads = queries.astype(jnp.float32).reshape(length, key_count, width).transpose(1, 0, 2)
    key_heads = keys.astype(jnp.float32).reshape(length, key_count, width).transpose(1, 0, 2)
    value_heads = (
        values.astype(jnp.float32).reshape(length, key_count, group, width).transpose(1, 2, 0, 3)
    )
    decay_logs = (
        jnp.log1p(-gate_code.astype(jnp.float32) * gate_step)
        .reshape(length, key_count, group)
        .transpose(1, 2, 0)
    )
    betas = (
        (beta_code.astype(jnp.float32) / beta_steps)
        .reshape(length, key_count, group)
        .transpose(1, 2, 0)
    )
    transition, local_state = jax.vmap(slab_effect)(key_heads, value_heads, decay_logs, betas)
    full_grad = lax.all_gather(out_grad, "head", axis=1, tiled=True)
    out_cot = jnp.dot(full_grad, w_out.T, preferred_element_type=jnp.float32)
    cot_heads = out_cot.reshape(length, key_count, group, width).transpose(1, 2, 0, 3)
    empty_states = jnp.zeros_like(transition)
    carried = jax.vmap(start_adjoint)(query_heads, key_heads, decay_logs, betas, cot_heads)
    transposed = jnp.swapaxes(transition, -1, -2)
    slabs = lax.axis_size("seq")

    def forward_turn(turn, arrived):
        return from_behind(matmul_states(transition, arrived) + local_state, "seq", 1)

    start_state = lax.fori_loop(0, slabs - 1, forward_turn, empty_states)

    def backward_turn(turn, arrived):
        return from_behind(matmul_states(transposed, arrived) + carried, "seq", -1)

    end_grad = lax.fori_loop(0, slabs - 1, backward_turn, empty_states)
    core_out, query_grad, key_grad, value_grad = jax.vmap(final_pass)(
        query_heads, key_heads, value_heads, decay_logs, betas, start_state, cot_heads, end_grad
    )
    attn_out = (
        core_out.transpose(2, 0, 1, 3)
        .reshape(length, key_count * group * width)
        .astype(jnp.bfloat16)
    )
    q_grad = query_grad.transpose(1, 0, 2).reshape(length, key_count * width)
    k_grad = key_grad.transpose(1, 0, 2).reshape(length, key_count * width)
    v_grad = value_grad.transpose(2, 0, 1, 3).reshape(length, key_count * group * width)
    scaling = (length * lax.axis_size("seq")) ** (-0.5)
    weight_grad = (
        lax.psum_scatter(
            jnp.dot(attn_out.T, full_grad, preferred_element_type=jnp.float32),
            "seq",
            scatter_dimension=0,
            tiled=True,
        )
        * scaling
    )
    return (attn_out, q_grad, k_grad, v_grad, weight_grad)


def solution(mesh):
    in_specs = (
        P("seq", "head"),
        P("seq", "head"),
        P("seq", "head"),
        P("seq", "head"),
        P("seq", "head"),
        P("seq", "head"),
        P("head", None),
    )
    out_specs = (
        P("seq", "head"),
        P("seq", "head"),
        P("seq", "head"),
        P("seq", "head"),
        P(("head", "seq"), None),
    )
    return jax.shard_map(
        per_device, mesh=mesh, in_specs=in_specs, out_specs=out_specs, check_vma=False
    )
```

profile of v0, /device:TPU:15, one launch (start us, length us, event | category | flops | bytes accessed | tf_op | source)
XLA Modules:
  0.0 706.4 jit_solution(11094657248866685844)
XLA Ops:
  11.9 25.9 %while.114 = (s32[]{:T(128)}, f32[1,2,128,128]{3,2,1,0:T(8,128)S(1)}, f32[1,2,128,128]{3,2,1,0:T(8,128)S(1)}, f32[2,1,2,64]{3,2,1,0:T(2,128)S(1)}, f32[2,1,64,12...) while((s32[]{:T(128)}, ...), condition=%wide.region_3.4_spmd.clone, body=%wide.region_1.3_spmd.clone.sunk | while | flops 132489408 | bytes 2056892 | solution.py:120
  12.8 9.8 %custom-call.41 = f32[1,2,1,64,64]{3,4,2,1,0:T(8,128)S(1)} custom-call(f32[1,2,1,64,64]{4,3,2,1,0:T(8,128)S(1)} %select_add_fusion.2), custom_call_target="InvertDiagBlocksLowerTriangular" | custom-call | tf_op jit(solution)/shard_map/vmap(vmap())/while/body/eval_jaxpr/triangular_solve | solution.py:100
  25.8 9.8 %custom-call.41 = f32[1,2,1,64,64]{3,4,2,1,0:T(8,128)S(1)} custom-call(f32[1,2,1,64,64]{4,3,2,1,0:T(8,128)S(1)} %select_add_fusion.2), custom_call_target="InvertDiagBlocksLowerTriangular" | custom-call | tf_op jit(solution)/shard_map/vmap(vmap())/while/body/eval_jaxpr/triangular_solve | solution.py:100
  38.0 266.0 %while.110 = (s32[]{:T(128)}, f32[1,2,128,128]{3,2,1,0:T(8,128)S(1)}, f32[1,2,128,128]{3,2,1,0:T(8,128)S(1)}, f32[1,2,128,128]{3,2,1,0:T(8,128)S(1)}, s32[]{:T(128)}) while((s32[]{:T(128)}, f32[1,2,128,128]{3,2,1,0:T(8,128)S(1)}, f32[1,2,128,128]{3,2,1,0:T(8,128)S(1)}, f32[1,2,128,128]{3,2,1,0:T(8,128)S(1)}, s32[]{:T(128)}) %tuple.218), condition=%wide.region_5.6_spmd, body=%wide.region_4.5_spmd.sunk | while | flops 50364416 | bytes 1048677 | solution.py:237
  122.2 6.5 collective-permute-start
  174.2 6.5 collective-permute-start
  226.3 6.5 collective-permute-start
  278.3 6.5 collective-permute-start
  304.0 25.6 %while.113 = (s32[]{:T(128)}, f32[1,2,128,128]{3,2,1,0:T(8,128)S(1)}, bf16[2,1,2,64,128]{4,3,0,2,1:T(8,128)(2,1)S(1)}, f32[2,1,128,64]{2,3,1,0:T(8,128)S(1)}, f3...) while((s32[]{:T(128)}, ...), condition=%wide.region_9.11_spmd.clone.clone, body=%wide.region_7.10_spmd.clone.clone.sunk | while | flops 113562048 | bytes 2285849 | solution.py:57
  304.9 9.8 %custom-call.40 = f32[1,2,1,64,64]{3,4,2,1,0:T(8,128)S(1)} custom-call(f32[1,2,1,64,64]{4,3,2,1,0:T(8,128)S(1)} %add_bitcast_fusion.7), custom_call_target="InvertDiagBlocksLowerTriangular" | custom-call | tf_op jit(solution)/shard_map/vmap(jvp(vmap()))/while/body/eval_jaxpr/triangular_solve/custom-call.0 | solution.py:45
  317.8 9.8 %custom-call.40 = f32[1,2,1,64,64]{3,4,2,1,0:T(8,128)S(1)} custom-call(f32[1,2,1,64,64]{4,3,2,1,0:T(8,128)S(1)} %add_bitcast_fusion.7), custom_call_target="InvertDiagBlocksLowerTriangular" | custom-call | tf_op jit(solution)/shard_map/vmap(jvp(vmap()))/while/body/eval_jaxpr/triangular_solve/custom-call.0 | solution.py:45
  329.7 32.1 %all_gather.3 = bf16[128,2048]{1,0:T(8,128)(2,1)S(1)} all-gather(bf16[128,128]{1,0:T(8,128)(2,1)S(1)} %copy-done.3), channel_id=1, replica_groups=mesh['seq'=32,'head'=16] {'head'}, dimensions={1}, use_global_device_ids=true | all-gather | bytes 557056 | tf_op jit(solution)/shard_map/all_gather | solution.py:226
  364.3 25.8 %while.115 = (s32[]{:T(128)}, f32[1,2,128,128]{3,2,1,0:T(8,128)S(1)}, f32[2,1,2,64]{3,2,1,0:T(2,128)S(1)}, f32[2,1,64,128]{3,2,1,0:T(8,128)S(1)}, f32[2,1,2,64]{...) while((s32[]{:T(128)}, ...), condition=%wide.region_12.14_spmd.clone, body=%wide.region_10.13_spmd.clone.sunk | while | flops 113586368 | bytes 1705664 | solution.py:173
  365.2 9.8 %custom-call.42 = f32[1,2,1,64,64]{3,4,2,1,0:T(8,128)S(1)} custom-call(f32[1,2,1,64,64]{4,3,2,1,0:T(8,128)S(1)} %add_bitcast_fusion.8), custom_call_target="InvertDiagBlocksLowerTriangular" | custom-call | tf_op jit(solution)/shard_map/vmap(vmap())/while/body/eval_jaxpr/triangular_solve/custom-call.0 | solution.py:153
  378.1 9.8 %custom-call.42 = f32[1,2,1,64,64]{3,4,2,1,0:T(8,128)S(1)} custom-call(f32[1,2,1,64,64]{4,3,2,1,0:T(8,128)S(1)} %add_bitcast_fusion.8), custom_call_target="InvertDiagBlocksLowerTriangular" | custom-call | tf_op jit(solution)/shard_map/vmap(vmap())/while/body/eval_jaxpr/triangular_solve/custom-call.0 | solution.py:153
  390.2 276.1 %while.111 = (s32[]{:T(128)}, f32[1,2,128,128]{3,2,1,0:T(8,128)S(1)}, f32[1,2,128,128]{3,2,1,0:T(8,128)S(1)}, f32[1,2,128,128]{3,2,1,0:T(8,128)S(1)}, s32[]{:T(128)}) while((s32[]{:T(128)}, f32[1,2,128,128]{3,2,1,0:T(8,128)S(1)}, f32[1,2,128,128]{3,2,1,0:T(8,128)S(1)}, f32[1,2,128,128]{3,2,1,0:T(8,128)S(1)}, s32[]{:T(128)}) %tuple.227), condition=%wide.region_14.16_spmd, body=%wide.region_13.15_spmd.sunk | while | flops 50364416 | bytes 1048677 | solution.py:242
  393.8 12.0 %collective-permute-done.1 = f32[1,2,128,128]{3,2,1,0:T(8,128)S(1)} collective-permute-done((f32[1,2,128,128]{3,2,1,0:T(8,128)S(1)}, f32[1,2,128,128]{3,2,1,0:T(8,128)S(1)}, u32[]{:S(2)}, u32[]{:S(2)}) %collective-permute-start.1) | collective-permute-done | bytes 131104 | tf_op jit(solution)/shard_map/while/body/eval_jaxpr/ppermute | solution.py:17
  425.4 6.5 collective-permute-done.1
  442.7 6.5 collective-permute-done.1
  451.4 6.6 collective-permute-done.1
  460.3 6.6 collective-permute-done.1
  666.6 28.2 %while.112 = (s32[]{:T(128)}, f32[1,2,128,128]{2,3,1,0:T(8,128)S(1)}, f32[2,1,64,128]{3,2,1,0:T(8,128)S(1)}, f32[2,1,64,128]{3,2,1,0:T(8,128)S(1)}, f32[2,1,2,64...) while((s32[]{:T(128)}, ...), condition=%wide.region_18.20_spmd.clone, body=%wide.region_15.19_spmd.clone.sunk | while | flops 233140288 | bytes 3349265 | solution.py:57
  667.3 9.8 %custom-call.39 = f32[1,2,1,64,64]{3,4,2,1,0:T(8,128)S(1)} custom-call(f32[1,2,1,64,64]{4,3,2,1,0:T(8,128)S(1)} %add_bitcast_fusion.6), custom_call_target="InvertDiagBlocksLowerTriangular" | custom-call | tf_op jit(solution)/shard_map/vmap(transpose(jvp(vmap())))/while/body/eval_jaxpr/triangular_solve | solution.py:45
  681.4 9.8 %custom-call.39 = f32[1,2,1,64,64]{3,4,2,1,0:T(8,128)S(1)} custom-call(f32[1,2,1,64,64]{4,3,2,1,0:T(8,128)S(1)} %add_bitcast_fusion.6), custom_call_target="InvertDiagBlocksLowerTriangular" | custom-call | tf_op jit(solution)/shard_map/vmap(transpose(jvp(vmap())))/while/body/eval_jaxpr/triangular_solve | solution.py:45
  (403 shorter events, 515.0 us)
Async XLA Ops:
  7.2 690.9 %reduce-scatter.2.cloned.1.call-start = ((), (), s32[]{:S(2)}) async-start(), calls=%async_computation.1 | async-start | bytes 2162688 | tf_op jit(solution)/shard_map/reduce_scatter | solution.py:256
  44.2 8.4 %collective-permute-start = (f32[1,2,128,128]{3,2,1,0:T(8,128)S(1)}, f32[1,2,128,128]{3,2,1,0:T(8,128)S(1)}, u32[]{:S(2)}, u32[]{:S(2)}) collective-permute-start(f32[1,2,128,128]{3,2,1,0:T(8,128)S(1)} %fusion.351), channel_id=1, source_target_pairs={{0,16},{16,32},{32,48},{48,64},{64,80},{80,96},{96,112},{112,128},... | collective-permute-start | bytes 393224 | tf_op jit(solution)/shard_map/while/body/eval_jaxpr/ppermute | solution.py:17
  61.5 8.4 %collective-permute-start = (f32[1,2,128,128]{3,2,1,0:T(8,128)S(1)}, f32[1,2,128,128]{3,2,1,0:T(8,128)S(1)}, u32[]{:S(2)}, u32[]{:S(2)}) collective-permute-start(f32[1,2,128,128]{3,2,1,0:T(8,128)S(1)} %fusion.351), channel_id=1, source_target_pairs={{0,16},{16,32},{32,48},{48,64},{64,80},{80,96},{96,112},{112,128},... | collective-permute-start | bytes 393224 | tf_op jit(solution)/shard_map/while/body/eval_jaxpr/ppermute | solution.py:17
  78.9 8.4 %collective-permute-start = (f32[1,2,128,128]{3,2,1,0:T(8,128)S(1)}, f32[1,2,128,128]{3,2,1,0:T(8,128)S(1)}, u32[]{:S(2)}, u32[]{:S(2)}) collective-permute-start(f32[1,2,128,128]{3,2,1,0:T(8,128)S(1)} %fusion.351), channel_id=1, source_target_pairs={{0,16},{16,32},{32,48},{48,64},{64,80},{80,96},{96,112},{112,128},... | collective-permute-start | bytes 393224 | tf_op jit(solution)/shard_map/while/body/eval_jaxpr/ppermute | solution.py:17
  87.5 8.4 %collective-permute-start = (f32[1,2,128,128]{3,2,1,0:T(8,128)S(1)}, f32[1,2,128,128]{3,2,1,0:T(8,128)S(1)}, u32[]{:S(2)}, u32[]{:S(2)}) collective-permute-start(f32[1,2,128,128]{3,2,1,0:T(8,128)S(1)} %fusion.351), channel_id=1, source_target_pairs={{0,16},{16,32},{32,48},{48,64},{64,80},{80,96},{96,112},{112,128},... | collective-permute-start | bytes 393224 | tf_op jit(solution)/shard_map/while/body/eval_jaxpr/ppermute | solution.py:17
  104.9 8.4 %collective-permute-start = (f32[1,2,128,128]{3,2,1,0:T(8,128)S(1)}, f32[1,2,128,128]{3,2,1,0:T(8,128)S(1)}, u32[]{:S(2)}, u32[]{:S(2)}) collective-permute-start(f32[1,2,128,128]{3,2,1,0:T(8,128)S(1)} %fusion.351), channel_id=1, source_target_pairs={{0,16},{16,32},{32,48},{48,64},{64,80},{80,96},{96,112},{112,128},... | collective-permute-start | bytes 393224 | tf_op jit(solution)/shard_map/while/body/eval_jaxpr/ppermute | solution.py:17
  113.5 8.4 %collective-permute-start = (f32[1,2,128,128]{3,2,1,0:T(8,128)S(1)}, f32[1,2,128,128]{3,2,1,0:T(8,128)S(1)}, u32[]{:S(2)}, u32[]{:S(2)}) collective-permute-start(f32[1,2,128,128]{3,2,1,0:T(8,128)S(1)} %fusion.351), channel_id=1, source_target_pairs={{0,16},{16,32},{32,48},{48,64},{64,80},{80,96},{96,112},{112,128},... | collective-permute-start | bytes 393224 | tf_op jit(solution)/shard_map/while/body/eval_jaxpr/ppermute | solution.py:17
  122.2 8.4 %collective-permute-start = (f32[1,2,128,128]{3,2,1,0:T(8,128)S(1)}, f32[1,2,128,128]{3,2,1,0:T(8,128)S(1)}, u32[]{:S(2)}, u32[]{:S(2)}) collective-permute-start(f32[1,2,128,128]{3,2,1,0:T(8,128)S(1)} %fusion.351), channel_id=1, source_target_pairs={{0,16},{16,32},{32,48},{48,64},{64,80},{80,96},{96,112},{112,128},... | collective-permute-start | bytes 393224 | tf_op jit(solution)/shard_map/while/body/eval_jaxpr/ppermute | solution.py:17
  130.9 8.4 %collective-permute-start = (f32[1,2,128,128]{3,2,1,0:T(8,128)S(1)}, f32[1,2,128,128]{3,2,1,0:T(8,128)S(1)}, u32[]{:S(2)}, u32[]{:S(2)}) collective-permute-start(f32[1,2,128,128]{3,2,1,0:T(8,128)S(1)} %fusion.351), channel_id=1, source_target_pairs={{0,16},{16,32},{32,48},{48,64},{64,80},{80,96},{96,112},{112,128},... | collective-permute-start | bytes 393224 | tf_op jit(solution)/shard_map/while/body/eval_jaxpr/ppermute | solution.py:17
  139.6 8.4 %collective-permute-start = (f32[1,2,128,128]{3,2,1,0:T(8,128)S(1)}, f32[1,2,128,128]{3,2,1,0:T(8,128)S(1)}, u32[]{:S(2)}, u32[]{:S(2)}) collective-permute-start(f32[1,2,128,128]{3,2,1,0:T(8,128)S(1)} %fusion.351), channel_id=1, source_target_pairs={{0,16},{16,32},{32,48},{48,64},{64,80},{80,96},{96,112},{112,128},... | collective-permute-start | bytes 393224 | tf_op jit(solution)/shard_map/while/body/eval_jaxpr/ppermute | solution.py:17
  156.9 8.4 %collective-permute-start = (f32[1,2,128,128]{3,2,1,0:T(8,128)S(1)}, f32[1,2,128,128]{3,2,1,0:T(8,128)S(1)}, u32[]{:S(2)}, u32[]{:S(2)}) collective-permute-start(f32[1,2,128,128]{3,2,1,0:T(8,128)S(1)} %fusion.351), channel_id=1, source_target_pairs={{0,16},{16,32},{32,48},{48,64},{64,80},{80,96},{96,112},{112,128},... | collective-permute-start | bytes 393224 | tf_op jit(solution)/shard_map/while/body/eval_jaxpr/ppermute | solution.py:17
  165.6 8.4 %collective-permute-start = (f32[1,2,128,128]{3,2,1,0:T(8,128)S(1)}, f32[1,2,128,128]{3,2,1,0:T(8,128)S(1)}, u32[]{:S(2)}, u32[]{:S(2)}) collective-permute-start(f32[1,2,128,128]{3,2,1,0:T(8,128)S(1)} %fusion.351), channel_id=1, source_target_pairs={{0,16},{16,32},{32,48},{48,64},{64,80},{80,96},{96,112},{112,128},... | collective-permute-start | bytes 393224 | tf_op jit(solution)/shard_map/while/body/eval_jaxpr/ppermute | solution.py:17
  174.2 8.4 %collective-permute-start = (f32[1,2,128,128]{3,2,1,0:T(8,128)S(1)}, f32[1,2,128,128]{3,2,1,0:T(8,128)S(1)}, u32[]{:S(2)}, u32[]{:S(2)}) collective-permute-start(f32[1,2,128,128]{3,2,1,0:T(8,128)S(1)} %fusion.351), channel_id=1, source_target_pairs={{0,16},{16,32},{32,48},{48,64},{64,80},{80,96},{96,112},{112,128},... | collective-permute-start | bytes 393224 | tf_op jit(solution)/shard_map/while/body/eval_jaxpr/ppermute | solution.py:17
  182.9 8.4 %collective-permute-start = (f32[1,2,128,128]{3,2,1,0:T(8,128)S(1)}, f32[1,2,128,128]{3,2,1,0:T(8,128)S(1)}, u32[]{:S(2)}, u32[]{:S(2)}) collective-permute-start(f32[1,2,128,128]{3,2,1,0:T(8,128)S(1)} %fusion.351), channel_id=1, source_target_pairs={{0,16},{16,32},{32,48},{48,64},{64,80},{80,96},{96,112},{112,128},... | collective-permute-start | bytes 393224 | tf_op jit(solution)/shard_map/while/body/eval_jaxpr/ppermute | solution.py:17
  191.6 8.4 %collective-permute-start = (f32[1,2,128,128]{3,2,1,0:T(8,128)S(1)}, f32[1,2,128,128]{3,2,1,0:T(8,128)S(1)}, u32[]{:S(2)}, u32[]{:S(2)}) collective-permute-start(f32[1,2,128,128]{3,2,1,0:T(8,128)S(1)} %fusion.351), channel_id=1, source_target_pairs={{0,16},{16,32},{32,48},{48,64},{64,80},{80,96},{96,112},{112,128},... | collective-permute-start | bytes 393224 | tf_op jit(solution)/shard_map/while/body/eval_jaxpr/ppermute | solution.py:17
  208.9 8.4 %collective-permute-start = (f32[1,2,128,128]{3,2,1,0:T(8,128)S(1)}, f32[1,2,128,128]{3,2,1,0:T(8,128)S(1)}, u32[]{:S(2)}, u32[]{:S(2)}) collective-permute-start(f32[1,2,128,128]{3,2,1,0:T(8,128)S(1)} %fusion.351), channel_id=1, source_target_pairs={{0,16},{16,32},{32,48},{48,64},{64,80},{80,96},{96,112},{112,128},... | collective-permute-start | bytes 393224 | tf_op jit(solution)/shard_map/while/body/eval_jaxpr/ppermute | solution.py:17
  226.3 8.4 %collective-permute-start = (f32[1,2,128,128]{3,2,1,0:T(8,128)S(1)}, f32[1,2,128,128]{3,2,1,0:T(8,128)S(1)}, u32[]{:S(2)}, u32[]{:S(2)}) collective-permute-start(f32[1,2,128,128]{3,2,1,0:T(8,128)S(1)} %fusion.351), channel_id=1, source_target_pairs={{0,16},{16,32},{32,48},{48,64},{64,80},{80,96},{96,112},{112,128},... | collective-permute-start | bytes 393224 | tf_op jit(solution)/shard_map/while/body/eval_jaxpr/ppermute | solution.py:17
  243.6 8.4 %collective-permute-start = (f32[1,2,128,128]{3,2,1,0:T(8,128)S(1)}, f32[1,2,128,128]{3,2,1,0:T(8,128)S(1)}, u32[]{:S(2)}, u32[]{:S(2)}) collective-permute-start(f32[1,2,128,128]{3,2,1,0:T(8,128)S(1)} %fusion.351), channel_id=1, source_target_pairs={{0,16},{16,32},{32,48},{48,64},{64,80},{80,96},{96,112},{112,128},... | collective-permute-start | bytes 393224 | tf_op jit(solution)/shard_map/while/body/eval_jaxpr/ppermute | solution.py:17
  278.3 8.4 %collective-permute-start = (f32[1,2,128,128]{3,2,1,0:T(8,128)S(1)}, f32[1,2,128,128]{3,2,1,0:T(8,128)S(1)}, u32[]{:S(2)}, u32[]{:S(2)}) collective-permute-start(f32[1,2,128,128]{3,2,1,0:T(8,128)S(1)} %fusion.351), channel_id=1, source_target_pairs={{0,16},{16,32},{32,48},{48,64},{64,80},{80,96},{96,112},{112,128},... | collective-permute-start | bytes 393224 | tf_op jit(solution)/shard_map/while/body/eval_jaxpr/ppermute | solution.py:17
  295.6 8.4 %collective-permute-start = (f32[1,2,128,128]{3,2,1,0:T(8,128)S(1)}, f32[1,2,128,128]{3,2,1,0:T(8,128)S(1)}, u32[]{:S(2)}, u32[]{:S(2)}) collective-permute-start(f32[1,2,128,128]{3,2,1,0:T(8,128)S(1)} %fusion.351), channel_id=1, source_target_pairs={{0,16},{16,32},{32,48},{48,64},{64,80},{80,96},{96,112},{112,128},... | collective-permute-start | bytes 393224 | tf_op jit(solution)/shard_map/while/body/eval_jaxpr/ppermute | solution.py:17
  390.5 15.3 %collective-permute-start.1 = (f32[1,2,128,128]{3,2,1,0:T(8,128)S(1)}, f32[1,2,128,128]{3,2,1,0:T(8,128)S(1)}, u32[]{:S(2)}, u32[]{:S(2)}) collective-permute-start(f32[1,2,128,128]{3,2,1,0:T(8,128)S(1)} %fusion.354), channel_id=1, source_target_pairs={{16,0},{32,16},{48,32},{64,48},{80,64},{96,80},{112,96},{128,112},... | collective-permute-start | bytes 393224 | tf_op jit(solution)/shard_map/while/body/eval_jaxpr/ppermute | solution.py:17
  423.4 8.4 %collective-permute-start.1 = (f32[1,2,128,128]{3,2,1,0:T(8,128)S(1)}, f32[1,2,128,128]{3,2,1,0:T(8,128)S(1)}, u32[]{:S(2)}, u32[]{:S(2)}) collective-permute-start(f32[1,2,128,128]{3,2,1,0:T(8,128)S(1)} %fusion.354), channel_id=1, source_target_pairs={{16,0},{32,16},{48,32},{64,48},{80,64},{96,80},{112,96},{128,112},... | collective-permute-start | bytes 393224 | tf_op jit(solution)/shard_map/while/body/eval_jaxpr/ppermute | solution.py:17
  449.5 8.6 %collective-permute-start.1 = (f32[1,2,128,128]{3,2,1,0:T(8,128)S(1)}, f32[1,2,128,128]{3,2,1,0:T(8,128)S(1)}, u32[]{:S(2)}, u32[]{:S(2)}) collective-permute-start(f32[1,2,128,128]{3,2,1,0:T(8,128)S(1)} %fusion.354), channel_id=1, source_target_pairs={{16,0},{32,16},{48,32},{64,48},{80,64},{96,80},{112,96},{128,112},... | collective-permute-start | bytes 393224 | tf_op jit(solution)/shard_map/while/body/eval_jaxpr/ppermute | solution.py:17
  458.3 8.6 %collective-permute-start.1 = (f32[1,2,128,128]{3,2,1,0:T(8,128)S(1)}, f32[1,2,128,128]{3,2,1,0:T(8,128)S(1)}, u32[]{:S(2)}, u32[]{:S(2)}) collective-permute-start(f32[1,2,128,128]{3,2,1,0:T(8,128)S(1)} %fusion.354), channel_id=1, source_target_pairs={{16,0},{32,16},{48,32},{64,48},{80,64},{96,80},{112,96},{128,112},... | collective-permute-start | bytes 393224 | tf_op jit(solution)/shard_map/while/body/eval_jaxpr/ppermute | solution.py:17
  (43 other events, 762.5 us)
Sparse Core Ops, SparseCore 0:
  363.8 101.0 reduce-scatter.1
where the time goes:
time: 709 us; the launch traced here: 706 us
  waiting for transfers between devices  266 us (38%)
  starting transfers between devices  259 us (37%)
  other arithmetic  89.1 us (13%)
  matrix products  38.5 us (5%)
  blocking collectives  32.1 us (5%)
  between operations  14.4 us (2%)
    ppermute x62, waiting for transfers between devices, from_behind(): lax.ppermute(value, axis, [(source, source + steps) for source in range(i...  266 us
    ppermute x62, starting transfers between devices, from_behind(): lax.ppermute(value, axis, [(source, source + steps) for source in range(i...  258 us
    another operation x16, other arithmetic, span_advance(): lax.linalg.triangular_solve(lower_mix, right_side, left_side=True, lower=...  39.9 us
    all_gather x1, blocking collectives, per_device(): full_grad = lax.all_gather(out_grad, 'head', axis=1, tiled=True)  32.1 us
    another operation x10, other arithmetic, retreat(): lax.linalg.triangular_solve(lower_mix, decay_cum[:, None] * key_block, le...  20 us
    another operation x8, other arithmetic, single_advance(): lax.linalg.triangular_solve(lower_mix, stacked, left_side=True, lower=Tru...  19.9 us
    dot_general x62, matrix products, matmul_states(): return jnp.einsum('abij,abjk->abik', left, right, precision=highest)  16.5 us
  transfers between devices with their start and end apart: 63, of which 62 were waited for; matrix products, arithmetic and copies ran while one was open for 9% of the time, Pallas kernels for 0%

commit v1 on v0

--- a/solution.py
+++ b/solution.py
@@ -9,6 +9,24 @@
 gate_step = 1e-06
 beta_steps = 256.0
 highest = lax.Precision.HIGHEST
+
+
+def gather_around(value, axis, dim):
+    ways, here, step = (lax.axis_size(axis), lax.axis_index(axis), value.shape[dim])
+    shape = [n * ways if d == dim else n for d, n in enumerate(value.shape)]
+    full = lax.dynamic_update_slice_in_dim(
+        jnp.zeros(shape, value.dtype), value, here * step, axis=dim
+    )
+    going_up = going_down = value
+    for far in range(1, ways // 2 + 1):
+        going_up = lax.ppermute(going_up, axis, [(d, (d + 1) % ways) for d in range(ways)])
+        full = lax.dynamic_update_slice_in_dim(full, going_up, (here - far) % ways * step, axis=dim)
+        if 2 * far < ways:
+            going_down = lax.ppermute(going_down, axis, [(d, (d - 1) % ways) for d in range(ways)])
+            full = lax.dynamic_update_slice_in_dim(
+                full, going_down, (here + far) % ways * step, axis=dim
+            )
+    return full
 
 
 def from_behind(value, axis, steps):
@@ -223,7 +241,7 @@
         .transpose(1, 2, 0)
     )
     transition, local_state = jax.vmap(slab_effect)(key_heads, value_heads, decay_logs, betas)
-    full_grad = lax.all_gather(out_grad, "head", axis=1, tiled=True)
+    full_grad = gather_around(out_grad, "head", 1)
     out_cot = jnp.dot(full_grad, w_out.T, preferred_element_type=jnp.float32)
     cot_heads = out_cot.reshape(length, key_count, group, width).transpose(1, 2, 0, 3)
     empty_states = jnp.zeros_like(transition)

time: 709 us -> 802 us (1.13)
  the two profiles are of different devices: /device:TPU:15 before, /device:TPU:2 now
where the time goes in v1:
time: 802 us; the launch traced here: 800 us
  waiting for transfers between devices  362 us (45%)
  starting transfers between devices  287 us (36%)
  other arithmetic  89 us (11%)
  matrix products  38.4 us (5%)
  between operations  15.1 us (2%)
    ppermute x62, waiting for transfers between devices, from_behind(): lax.ppermute(value, axis, [(source, source + steps) for source in range(i...  267 us
    ppermute x62, starting transfers between devices, from_behind(): lax.ppermute(value, axis, [(source, source + steps) for source in range(i...  229 us
    reduce_scatter x1, waiting for transfers between devices, per_device(): lax.psum_scatter(jnp.dot(attn_out.T, full_grad, preferred_element_type=jn...  90 us
    ppermute x7, starting transfers between devices, gather_around(): lax.ppermute(going_down, axis, [(d, (d - 1) % ways) for d in range(ways)])  40.3 us
    another operation x16, other arithmetic, span_advance(): lax.linalg.triangular_solve(lower_mix, right_side, left_side=True, lower=...  39.9 us
    another operation x10, other arithmetic, retreat(): lax.linalg.triangular_solve(lower_mix, decay_cum[:, None] * key_block, le...  20.1 us
    another operation x8, other arithmetic, single_advance(): lax.linalg.triangular_solve(lower_mix, stacked, left_side=True, lower=Tru...  19.9 us
    ppermute x8, starting transfers between devices, gather_around(): lax.ppermute(going_up, axis, [(d, (d + 1) % ways) for d in range(ways)])  17.6 us
  transfers between devices with their start and end apart: 78, of which 64 were waited for; matrix products, arithmetic and copies ran while one was open for 12% of the time, Pallas kernels for 0%

profile of v1, /device:TPU:2, one launch (start us, length us, event | category | flops | bytes accessed | tf_op | source)
XLA Modules:
  0.0 799.7 jit_solution(17038747528002987283)
XLA Ops:
  11.2 9.5 %collective-permute-start.3 = (bf16[128,128]{1,0:T(8,128)(2,1)}, bf16[128,128]{1,0:T(8,128)(2,1)S(1)}, u32[]{:S(2)}, u32[]{:S(2)}) collective-permute-start(bf16[128,128]{1,0:T(8,128)(2,1)} %param.26), channel_id=1, source_target_pairs={{0,15},{1,0},{2,1},{3,2},{4,3},{5,4},{6,5},{7,6},{8,7},{9,8},{10,9... | collective-permute-start | bytes 98312 | tf_op jit(solution)/shard_map/ppermute | solution.py:25
  25.3 25.9 %while.114 = (s32[]{:T(128)}, f32[1,2,128,128]{3,2,1,0:T(8,128)S(1)}, f32[1,2,128,128]{3,2,1,0:T(8,128)S(1)}, f32[2,1,2,64]{3,2,1,0:T(2,128)S(1)}, f32[2,1,64,12...) while((s32[]{:T(128)}, ...), condition=%wide.region_3.4_spmd.clone, body=%wide.region_1.3_spmd.clone.sunk | while | flops 132489408 | bytes 2056900 | solution.py:138
  26.3 9.8 %custom-call.41 = f32[1,2,1,64,64]{3,4,2,1,0:T(8,128)S(1)} custom-call(f32[1,2,1,64,64]{4,3,2,1,0:T(8,128)S(1)} %select_add_fusion.2), custom_call_target="InvertDiagBlocksLowerTriangular" | custom-call | tf_op jit(solution)/shard_map/vmap(vmap())/while/body/eval_jaxpr/triangular_solve | solution.py:118
  39.3 9.8 %custom-call.41 = f32[1,2,1,64,64]{3,4,2,1,0:T(8,128)S(1)} custom-call(f32[1,2,1,64,64]{4,3,2,1,0:T(8,128)S(1)} %select_add_fusion.2), custom_call_target="InvertDiagBlocksLowerTriangular" | custom-call | tf_op jit(solution)/shard_map/vmap(vmap())/while/body/eval_jaxpr/triangular_solve | solution.py:118
  51.4 243.1 %while.110 = (s32[]{:T(128)}, f32[1,2,128,128]{3,2,1,0:T(8,128)S(1)}, f32[1,2,128,128]{3,2,1,0:T(8,128)S(1)}, f32[1,2,128,128]{3,2,1,0:T(8,128)S(1)}, s32[]{:T(128)}) while((s32[]{:T(128)}, f32[1,2,128,128]{3,2,1,0:T(8,128)S(1)}, f32[1,2,128,128]{3,2,1,0:T(8,128)S(1)}, f32[1,2,128,128]{3,2,1,0:T(8,128)S(1)}, s32[]{:T(128)}) %tuple.218), condition=%wide.region_5.6_spmd, body=%wide.region_4.5_spmd.sunk | while | flops 50364416 | bytes 1048677 | solution.py:255
  156.1 7.4 collective-permute-start
  208.1 7.4 collective-permute-start
  234.1 7.4 collective-permute-start
  260.1 7.4 collective-permute-start
  286.2 7.4 collective-permute-start
  294.6 25.7 %while.113 = (s32[]{:T(128)}, f32[1,2,128,128]{3,2,1,0:T(8,128)S(1)}, bf16[2,1,2,64,128]{4,3,0,2,1:T(8,128)(2,1)S(1)}, f32[2,1,128,64]{2,3,1,0:T(8,128)S(1)}, f3...) while((s32[]{:T(128)}, ...), condition=%wide.region_9.11_spmd.clone.clone, body=%wide.region_7.10_spmd.clone.clone.sunk | while | flops 113562048 | bytes 2285857 | solution.py:75
  295.7 9.8 %custom-call.40 = f32[1,2,1,64,64]{3,4,2,1,0:T(8,128)S(1)} custom-call(f32[1,2,1,64,64]{4,3,2,1,0:T(8,128)S(1)} %add_bitcast_fusion.7), custom_call_target="InvertDiagBlocksLowerTriangular" | custom-call | tf_op jit(solution)/shard_map/vmap(jvp(vmap()))/while/body/eval_jaxpr/triangular_solve/custom-call.0 | solution.py:63
  308.5 9.8 %custom-call.40 = f32[1,2,1,64,64]{3,4,2,1,0:T(8,128)S(1)} custom-call(f32[1,2,1,64,64]{4,3,2,1,0:T(8,128)S(1)} %add_bitcast_fusion.7), custom_call_target="InvertDiagBlocksLowerTriangular" | custom-call | tf_op jit(solution)/shard_map/vmap(jvp(vmap()))/while/body/eval_jaxpr/triangular_solve/custom-call.0 | solution.py:63
  373.9 25.8 %while.115 = (s32[]{:T(128)}, f32[1,2,128,128]{3,2,1,0:T(8,128)S(1)}, f32[2,1,2,64]{3,2,1,0:T(2,128)S(1)}, f32[2,1,64,128]{3,2,1,0:T(8,128)S(1)}, f32[2,1,2,64]{...) while((s32[]{:T(128)}, ...), condition=%wide.region_12.14_spmd.clone, body=%wide.region_10.13_spmd.clone.sunk | while | flops 113586368 | bytes 1705672 | solution.py:191
  374.9 9.8 %custom-call.42 = f32[1,2,1,64,64]{3,4,2,1,0:T(8,128)S(1)} custom-call(f32[1,2,1,64,64]{4,3,2,1,0:T(8,128)S(1)} %add_bitcast_fusion.8), custom_call_target="InvertDiagBlocksLowerTriangular" | custom-call | tf_op jit(solution)/shard_map/vmap(vmap())/while/body/eval_jaxpr/triangular_solve/custom-call.0 | solution.py:171
  387.8 9.8 %custom-call.42 = f32[1,2,1,64,64]{3,4,2,1,0:T(8,128)S(1)} custom-call(f32[1,2,1,64,64]{4,3,2,1,0:T(8,128)S(1)} %add_bitcast_fusion.8), custom_call_target="InvertDiagBlocksLowerTriangular" | custom-call | tf_op jit(solution)/shard_map/vmap(vmap())/while/body/eval_jaxpr/triangular_solve/custom-call.0 | solution.py:171
  399.8 270.7 %while.111 = (s32[]{:T(128)}, f32[1,2,128,128]{3,2,1,0:T(8,128)S(1)}, f32[1,2,128,128]{3,2,1,0:T(8,128)S(1)}, f32[1,2,128,128]{3,2,1,0:T(8,128)S(1)}, s32[]{:T(128)}) while((s32[]{:T(128)}, f32[1,2,128,128]{3,2,1,0:T(8,128)S(1)}, f32[1,2,128,128]{3,2,1,0:T(8,128)S(1)}, f32[1,2,128,128]{3,2,1,0:T(8,128)S(1)}, s32[]{:T(128)}) %tuple.227), condition=%wide.region_14.16_spmd, body=%wide.region_13.15_spmd.sunk | while | flops 50364416 | bytes 1048677 | solution.py:260
  408.6 9.1 %collective-permute-done.1 = f32[1,2,128,128]{3,2,1,0:T(8,128)S(1)} collective-permute-done((f32[1,2,128,128]{3,2,1,0:T(8,128)S(1)}, f32[1,2,128,128]{3,2,1,0:T(8,128)S(1)}, u32[]{:S(2)}, u32[]{:S(2)}) %collective-permute-start.1) | collective-permute-done | bytes 131104 | tf_op jit(solution)/shard_map/while/body/eval_jaxpr/ppermute | solution.py:35
  426.5 9.2 %collective-permute-done.1 = f32[1,2,128,128]{3,2,1,0:T(8,128)S(1)} collective-permute-done((f32[1,2,128,128]{3,2,1,0:T(8,128)S(1)}, f32[1,2,128,128]{3,2,1,0:T(8,128)S(1)}, u32[]{:S(2)}, u32[]{:S(2)}) %collective-permute-start.1) | collective-permute-done | bytes 131104 | tf_op jit(solution)/shard_map/while/body/eval_jaxpr/ppermute | solution.py:35
  444.4 9.3 %collective-permute-done.1 = f32[1,2,128,128]{3,2,1,0:T(8,128)S(1)} collective-permute-done((f32[1,2,128,128]{3,2,1,0:T(8,128)S(1)}, f32[1,2,128,128]{3,2,1,0:T(8,128)S(1)}, u32[]{:S(2)}, u32[]{:S(2)}) %collective-permute-start.1) | collective-permute-done | bytes 131104 | tf_op jit(solution)/shard_map/while/body/eval_jaxpr/ppermute | solution.py:35
  670.7 28.2 %while.112 = (s32[]{:T(128)}, f32[1,2,128,128]{2,3,1,0:T(8,128)S(1)}, f32[2,1,64,128]{3,2,1,0:T(8,128)S(1)}, f32[2,1,64,128]{3,2,1,0:T(8,128)S(1)}, f32[2,1,2,64...) while((s32[]{:T(128)}, ...), condition=%wide.region_18.20_spmd.clone, body=%wide.region_15.19_spmd.clone.sunk | while | flops 233140288 | bytes 3349273 | solution.py:75
  671.6 9.8 %custom-call.39 = f32[1,2,1,64,64]{3,4,2,1,0:T(8,128)S(1)} custom-call(f32[1,2,1,64,64]{4,3,2,1,0:T(8,128)S(1)} %add_bitcast_fusion.6), custom_call_target="InvertDiagBlocksLowerTriangular" | custom-call | tf_op jit(solution)/shard_map/vmap(transpose(jvp(vmap())))/while/body/eval_jaxpr/triangular_solve | solution.py:63
  685.7 9.8 %custom-call.39 = f32[1,2,1,64,64]{3,4,2,1,0:T(8,128)S(1)} custom-call(f32[1,2,1,64,64]{4,3,2,1,0:T(8,128)S(1)} %add_bitcast_fusion.6), custom_call_target="InvertDiagBlocksLowerTriangular" | custom-call | tf_op jit(solution)/shard_map/vmap(transpose(jvp(vmap())))/while/body/eval_jaxpr/triangular_solve | solution.py:63
  701.4 90.0 %reduce-scatter.2.cloned.1.call-done = f32[8,2048]{1,0:T(8,128)} async-done(((f32[256,2048]{1,0:T(8,128)}), f32[8,2048]{1,0:T(8,128)}) %reduce-scatter.2.cloned.1.call-update) | async-done | bytes 65552 | tf_op jit(solution)/shard_map/reduce_scatter | solution.py:274
  (449 shorter events, 539.6 us)
Async XLA Ops:
  7.2 784.2 %reduce-scatter.2.cloned.1.call-start = ((), (), s32[]{:S(2)}) async-start(), calls=%async_computation.1 | async-start | bytes 2162688 | tf_op jit(solution)/shard_map/reduce_scatter | solution.py:274
  7.2 314.5 %collective-permute-start.2 = (bf16[128,128]{1,0:T(8,128)(2,1)}, bf16[128,128]{1,0:T(8,128)(2,1)S(1)}, u32[]{:S(2)}, u32[]{:S(2)}) collective-permute-start(bf16[128,128]{1,0:T(8,128)(2,1)} %param.26), channel_id=1, source_target_pairs={{0,1},{1,2},{2,3},{3,4},{4,5},{5,6},{6,7},{7,8},{8,9},{9,10},{10,1... | collective-permute-start | bytes 98312 | tf_op jit(solution)/shard_map/ppermute | solution.py:22
  11.2 312.4 %collective-permute-start.3 = (bf16[128,128]{1,0:T(8,128)(2,1)}, bf16[128,128]{1,0:T(8,128)(2,1)S(1)}, u32[]{:S(2)}, u32[]{:S(2)}) collective-permute-start(bf16[128,128]{1,0:T(8,128)(2,1)} %param.26), channel_id=1, source_target_pairs={{0,15},{1,0},{2,1},{3,2},{4,3},{5,4},{6,5},{7,6},{8,7},{9,8},{10,9... | collective-permute-start | bytes 98312 | tf_op jit(solution)/shard_map/ppermute | solution.py:25
  138.7 8.4 %collective-permute-start = (f32[1,2,128,128]{3,2,1,0:T(8,128)S(1)}, f32[1,2,128,128]{3,2,1,0:T(8,128)S(1)}, u32[]{:S(2)}, u32[]{:S(2)}) collective-permute-start(f32[1,2,128,128]{3,2,1,0:T(8,128)S(1)} %fusion.351), channel_id=1, source_target_pairs={{0,16},{16,32},{32,48},{48,64},{64,80},{80,96},{96,112},{112,128},... | collective-permute-start | bytes 393224 | tf_op jit(solution)/shard_map/while/body/eval_jaxpr/ppermute | solution.py:35
  156.1 8.4 %collective-permute-start = (f32[1,2,128,128]{3,2,1,0:T(8,128)S(1)}, f32[1,2,128,128]{3,2,1,0:T(8,128)S(1)}, u32[]{:S(2)}, u32[]{:S(2)}) collective-permute-start(f32[1,2,128,128]{3,2,1,0:T(8,128)S(1)} %fusion.351), channel_id=1, source_target_pairs={{0,16},{16,32},{32,48},{48,64},{64,80},{80,96},{96,112},{112,128},... | collective-permute-start | bytes 393224 | tf_op jit(solution)/shard_map/while/body/eval_jaxpr/ppermute | solution.py:35
  164.8 8.4 %collective-permute-start = (f32[1,2,128,128]{3,2,1,0:T(8,128)S(1)}, f32[1,2,128,128]{3,2,1,0:T(8,128)S(1)}, u32[]{:S(2)}, u32[]{:S(2)}) collective-permute-start(f32[1,2,128,128]{3,2,1,0:T(8,128)S(1)} %fusion.351), channel_id=1, source_target_pairs={{0,16},{16,32},{32,48},{48,64},{64,80},{80,96},{96,112},{112,128},... | collective-permute-start | bytes 393224 | tf_op jit(solution)/shard_map/while/body/eval_jaxpr/ppermute | solution.py:35
  182.1 8.4 %collective-permute-start = (f32[1,2,128,128]{3,2,1,0:T(8,128)S(1)}, f32[1,2,128,128]{3,2,1,0:T(8,128)S(1)}, u32[]{:S(2)}, u32[]{:S(2)}) collective-permute-start(f32[1,2,128,128]{3,2,1,0:T(8,128)S(1)} %fusion.351), channel_id=1, source_target_pairs={{0,16},{16,32},{32,48},{48,64},{64,80},{80,96},{96,112},{112,128},... | collective-permute-start | bytes 393224 | tf_op jit(solution)/shard_map/while/body/eval_jaxpr/ppermute | solution.py:35
  190.8 8.4 %collective-permute-start = (f32[1,2,128,128]{3,2,1,0:T(8,128)S(1)}, f32[1,2,128,128]{3,2,1,0:T(8,128)S(1)}, u32[]{:S(2)}, u32[]{:S(2)}) collective-permute-start(f32[1,2,128,128]{3,2,1,0:T(8,128)S(1)} %fusion.351), channel_id=1, source_target_pairs={{0,16},{16,32},{32,48},{48,64},{64,80},{80,96},{96,112},{112,128},... | collective-permute-start | bytes 393224 | tf_op jit(solution)/shard_map/while/body/eval_jaxpr/ppermute | solution.py:35
  208.1 8.4 %collective-permute-start = (f32[1,2,128,128]{3,2,1,0:T(8,128)S(1)}, f32[1,2,128,128]{3,2,1,0:T(8,128)S(1)}, u32[]{:S(2)}, u32[]{:S(2)}) collective-permute-start(f32[1,2,128,128]{3,2,1,0:T(8,128)S(1)} %fusion.351), channel_id=1, source_target_pairs={{0,16},{16,32},{32,48},{48,64},{64,80},{80,96},{96,112},{112,128},... | collective-permute-start | bytes 393224 | tf_op jit(solution)/shard_map/while/body/eval_jaxpr/ppermute | solution.py:35
  216.8 8.4 %collective-permute-start = (f32[1,2,128,128]{3,2,1,0:T(8,128)S(1)}, f32[1,2,128,128]{3,2,1,0:T(8,128)S(1)}, u32[]{:S(2)}, u32[]{:S(2)}) collective-permute-start(f32[1,2,128,128]{3,2,1,0:T(8,128)S(1)} %fusion.351), channel_id=1, source_target_pairs={{0,16},{16,32},{32,48},{48,64},{64,80},{80,96},{96,112},{112,128},... | collective-permute-start | bytes 393224 | tf_op jit(solution)/shard_map/while/body/eval_jaxpr/ppermute | solution.py:35
  234.1 8.4 %collective-permute-start = (f32[1,2,128,128]{3,2,1,0:T(8,128)S(1)}, f32[1,2,128,128]{3,2,1,0:T(8,128)S(1)}, u32[]{:S(2)}, u32[]{:S(2)}) collective-permute-start(f32[1,2,128,128]{3,2,1,0:T(8,128)S(1)} %fusion.351), channel_id=1, source_target_pairs={{0,16},{16,32},{32,48},{48,64},{64,80},{80,96},{96,112},{112,128},... | collective-permute-start | bytes 393224 | tf_op jit(solution)/shard_map/while/body/eval_jaxpr/ppermute | solution.py:35
  242.8 8.4 %collective-permute-start = (f32[1,2,128,128]{3,2,1,0:T(8,128)S(1)}, f32[1,2,128,128]{3,2,1,0:T(8,128)S(1)}, u32[]{:S(2)}, u32[]{:S(2)}) collective-permute-start(f32[1,2,128,128]{3,2,1,0:T(8,128)S(1)} %fusion.351), channel_id=1, source_target_pairs={{0,16},{16,32},{32,48},{48,64},{64,80},{80,96},{96,112},{112,128},... | collective-permute-start | bytes 393224 | tf_op jit(solution)/shard_map/while/body/eval_jaxpr/ppermute | solution.py:35
  260.1 8.4 %collective-permute-start = (f32[1,2,128,128]{3,2,1,0:T(8,128)S(1)}, f32[1,2,128,128]{3,2,1,0:T(8,128)S(1)}, u32[]{:S(2)}, u32[]{:S(2)}) collective-permute-start(f32[1,2,128,128]{3,2,1,0:T(8,128)S(1)} %fusion.351), channel_id=1, source_target_pairs={{0,16},{16,32},{32,48},{48,64},{64,80},{80,96},{96,112},{112,128},... | collective-permute-start | bytes 393224 | tf_op jit(solution)/shard_map/while/body/eval_jaxpr/ppermute | solution.py:35
  268.8 8.4 %collective-permute-start = (f32[1,2,128,128]{3,2,1,0:T(8,128)S(1)}, f32[1,2,128,128]{3,2,1,0:T(8,128)S(1)}, u32[]{:S(2)}, u32[]{:S(2)}) collective-permute-start(f32[1,2,128,128]{3,2,1,0:T(8,128)S(1)} %fusion.351), channel_id=1, source_target_pairs={{0,16},{16,32},{32,48},{48,64},{64,80},{80,96},{96,112},{112,128},... | collective-permute-start | bytes 393224 | tf_op jit(solution)/shard_map/while/body/eval_jaxpr/ppermute | solution.py:35
  286.2 8.4 %collective-permute-start = (f32[1,2,128,128]{3,2,1,0:T(8,128)S(1)}, f32[1,2,128,128]{3,2,1,0:T(8,128)S(1)}, u32[]{:S(2)}, u32[]{:S(2)}) collective-permute-start(f32[1,2,128,128]{3,2,1,0:T(8,128)S(1)} %fusion.351), channel_id=1, source_target_pairs={{0,16},{16,32},{32,48},{48,64},{64,80},{80,96},{96,112},{112,128},... | collective-permute-start | bytes 393224 | tf_op jit(solution)/shard_map/while/body/eval_jaxpr/ppermute | solution.py:35
  404.8 12.9 %collective-permute-start.1 = (f32[1,2,128,128]{3,2,1,0:T(8,128)S(1)}, f32[1,2,128,128]{3,2,1,0:T(8,128)S(1)}, u32[]{:S(2)}, u32[]{:S(2)}) collective-permute-start(f32[1,2,128,128]{3,2,1,0:T(8,128)S(1)} %fusion.354), channel_id=1, source_target_pairs={{16,0},{32,16},{48,32},{64,48},{80,64},{96,80},{112,96},{128,112},... | collective-permute-start | bytes 393224 | tf_op jit(solution)/shard_map/while/body/eval_jaxpr/ppermute | solution.py:35
  424.6 11.1 %collective-permute-start.1 = (f32[1,2,128,128]{3,2,1,0:T(8,128)S(1)}, f32[1,2,128,128]{3,2,1,0:T(8,128)S(1)}, u32[]{:S(2)}, u32[]{:S(2)}) collective-permute-start(f32[1,2,128,128]{3,2,1,0:T(8,128)S(1)} %fusion.354), channel_id=1, source_target_pairs={{16,0},{32,16},{48,32},{64,48},{80,64},{96,80},{112,96},{128,112},... | collective-permute-start | bytes 393224 | tf_op jit(solution)/shard_map/while/body/eval_jaxpr/ppermute | solution.py:35
  442.5 11.2 %collective-permute-start.1 = (f32[1,2,128,128]{3,2,1,0:T(8,128)S(1)}, f32[1,2,128,128]{3,2,1,0:T(8,128)S(1)}, u32[]{:S(2)}, u32[]{:S(2)}) collective-permute-start(f32[1,2,128,128]{3,2,1,0:T(8,128)S(1)} %fusion.354), channel_id=1, source_target_pairs={{16,0},{32,16},{48,32},{64,48},{80,64},{96,80},{112,96},{128,112},... | collective-permute-start | bytes 393224 | tf_op jit(solution)/shard_map/while/body/eval_jaxpr/ppermute | solution.py:35
  471.3 8.4 %collective-permute-start.1 = (f32[1,2,128,128]{3,2,1,0:T(8,128)S(1)}, f32[1,2,128,128]{3,2,1,0:T(8,128)S(1)}, u32[]{:S(2)}, u32[]{:S(2)}) collective-permute-start(f32[1,2,128,128]{3,2,1,0:T(8,128)S(1)} %fusion.354), channel_id=1, source_target_pairs={{16,0},{32,16},{48,32},{64,48},{80,64},{96,80},{112,96},{128,112},... | collective-permute-start | bytes 393224 | tf_op jit(solution)/shard_map/while/body/eval_jaxpr/ppermute | solution.py:35
  480.0 8.4 %collective-permute-start.1 = (f32[1,2,128,128]{3,2,1,0:T(8,128)S(1)}, f32[1,2,128,128]{3,2,1,0:T(8,128)S(1)}, u32[]{:S(2)}, u32[]{:S(2)}) collective-permute-start(f32[1,2,128,128]{3,2,1,0:T(8,128)S(1)} %fusion.354), channel_id=1, source_target_pairs={{16,0},{32,16},{48,32},{64,48},{80,64},{96,80},{112,96},{128,112},... | collective-permute-start | bytes 393224 | tf_op jit(solution)/shard_map/while/body/eval_jaxpr/ppermute | solution.py:35
  523.3 8.4 %collective-permute-start.1 = (f32[1,2,128,128]{3,2,1,0:T(8,128)S(1)}, f32[1,2,128,128]{3,2,1,0:T(8,128)S(1)}, u32[]{:S(2)}, u32[]{:S(2)}) collective-permute-start(f32[1,2,128,128]{3,2,1,0:T(8,128)S(1)} %fusion.354), channel_id=1, source_target_pairs={{16,0},{32,16},{48,32},{64,48},{80,64},{96,80},{112,96},{128,112},... | collective-permute-start | bytes 393224 | tf_op jit(solution)/shard_map/while/body/eval_jaxpr/ppermute | solution.py:35
  532.0 8.4 %collective-permute-start.1 = (f32[1,2,128,128]{3,2,1,0:T(8,128)S(1)}, f32[1,2,128,128]{3,2,1,0:T(8,128)S(1)}, u32[]{:S(2)}, u32[]{:S(2)}) collective-permute-start(f32[1,2,128,128]{3,2,1,0:T(8,128)S(1)} %fusion.354), channel_id=1, source_target_pairs={{16,0},{32,16},{48,32},{64,48},{80,64},{96,80},{112,96},{128,112},... | collective-permute-start | bytes 393224 | tf_op jit(solution)/shard_map/while/body/eval_jaxpr/ppermute | solution.py:35
  584.0 8.4 %collective-permute-start.1 = (f32[1,2,128,128]{3,2,1,0:T(8,128)S(1)}, f32[1,2,128,128]{3,2,1,0:T(8,128)S(1)}, u32[]{:S(2)}, u32[]{:S(2)}) collective-permute-start(f32[1,2,128,128]{3,2,1,0:T(8,128)S(1)} %fusion.354), channel_id=1, source_target_pairs={{16,0},{32,16},{48,32},{64,48},{80,64},{96,80},{112,96},{128,112},... | collective-permute-start | bytes 393224 | tf_op jit(solution)/shard_map/while/body/eval_jaxpr/ppermute | solution.py:35
  636.1 8.4 %collective-permute-start.1 = (f32[1,2,128,128]{3,2,1,0:T(8,128)S(1)}, f32[1,2,128,128]{3,2,1,0:T(8,128)S(1)}, u32[]{:S(2)}, u32[]{:S(2)}) collective-permute-start(f32[1,2,128,128]{3,2,1,0:T(8,128)S(1)} %fusion.354), channel_id=1, source_target_pairs={{16,0},{32,16},{48,32},{64,48},{80,64},{96,80},{112,96},{128,112},... | collective-permute-start | bytes 393224 | tf_op jit(solution)/shard_map/while/body/eval_jaxpr/ppermute | solution.py:35
  (58 other events, 850.2 us)
Sparse Core Ops, SparseCore 0:
  670.7 120.6 reduce-scatter.1
